TPU v7x, 32 devices: a whole 2x2x4 slice. The times are simulated.
32 devices in a mesh: dp: 8 (over z, y), rep: 4 (over x, core).
Axes of the slice: x: 2, y: 2, z: 4, core: 2. Of those that a mesh axis runs over, the one named last changes fastest.
Arguments:
- image_tokens: bfloat16 [256, 50, 768], P(('dp', 'rep')), may hold values from -6 to 6
- image_weights: bfloat16 [768, 9216], P('dp'), may hold values from -1 to 1
- image_vectors: float32 [9216], replicated, may hold values from -0.8 to 1.4
- text_tokens: bfloat16 [64, 64, 768], P(('dp', 'rep')), may hold values from -6 to 6
- segments: int32 [64, 64], P(('dp', 'rep')), may hold values from 0 to 3, never falling along the last dimension, each value on 1 to 28 neighbouring positions
- text_weights: float32 [768, 9216], P('dp'), may hold values from -1 to 1
- text_vectors: float32 [9216], replicated, may hold values from -0.8 to 1.4
- momentum: float32 [768, 9216], P('dp'), may hold values from -0.5 to 0.5
- vector_momentum: float32 [9216], replicated, may hold values from -2.5 to 2.5
- error_feedback: float32 [4, 768, 9216], P('rep', 'dp'), may hold values from -2.5 to 2.5
- start_factors: float32 [8, 9216], replicated, may hold values from -6 to 6
Outputs:
- contrast_loss: float32 [], replicated
- text_output: float32 [64, 64, 768], P(('dp', 'rep'))
- text_input_grad: float32 [64, 64, 768], P(('dp', 'rep'))
- new_weights: float32 [768, 9216], P('dp')
- new_momentum: float32 [768, 9216], P('dp')
- new_feedback: float32 [4, 768, 9216], P('rep', 'dp')
- new_vectors: float32 [9216], replicated
- new_vector_momentum: float32 [9216], replicated
- left_factors: float32 [32, 768], replicated
- right_factors: float32 [8, 9216], replicated
Inputs may be any that keep to these rules, and one draw needn't show every extreme that they name: `segments`: each row holds 4 captions numbered in order, each of 1 to 28 tokens, some caption of exactly 28.
All inputs are finite; a program needn't handle non-finite values.
Results may differ from a plain program's by a relative error of at most 0.015.
The roundings to bfloat16 on the way count: a program that leaves them out, or rounds other values in their place, can miss the bound.
Values may be sent and summed in bfloat16 or wider, within the bound.
A program may use at most 192 MiB of HBM per device.

v0:
```python
import jax
import jax.numpy as jnp
from jax import lax
from jax.sharding import PartitionSpec as P

D = 768
FF = 3072
HEADS = 12
HEAD_DIM = 64
PER_ROW = 4
PRECISE = lax.Precision.HIGHEST
LAYER_EPS = 1e-06
SCORE_SCALE = 0.125
LOGIT_SCALE = 50.0
MOMENTUM_DECAY = 0.9
STEP_RATE = 0.08
NORM_FLOOR = 1e-08
MASKED = -1e30


def layer_norm(values, layer_gain, layer_shift):
    center = values - jnp.mean(values, axis=-1, keepdims=True)
    spread = jnp.mean(center * center, axis=-1, keepdims=True)
    return center * lax.rsqrt(spread + LAYER_EPS) * layer_gain + layer_shift


def unit_rows(values):
    return values * lax.rsqrt(jnp.sum(values * values, axis=-1, keepdims=True) + LAYER_EPS)


def vector_parts(vectors):
    pieces = [vectors[position * D : (position + 1) * D] for position in range(8)]
    return pieces + [vectors[8 * D :]]


def matrix_bounds():
    return ((0, 3 * D), (3 * D, 4 * D), (4 * D, 4 * D + FF), (4 * D + FF, 4 * D + 2 * FF))


def row_log_total(values):
    highest = jnp.max(values, axis=1, keepdims=True)
    return highest[:, 0] + jnp.log(jnp.sum(jnp.exp(values - highest), axis=1))


def masked_scores(query_heads, key_heads, allowed):
    scores = (
        jnp.einsum("rshd,rthd->rhst", query_heads, key_heads, preferred_element_type=jnp.float32)
        * SCORE_SCALE
    )
    return jnp.where(allowed[:, None], scores, MASKED)


def block_forward(inputs, allowed, weights, vector_pieces):
    (
        gain_one,
        shift_one,
        bias_query,
        bias_value,
        bias_out,
        gain_two,
        shift_two,
        bias_shrink,
        bias_expand,
    ) = vector_pieces
    row_count, seq_tokens = (inputs.shape[0], inputs.shape[1])
    normed = layer_norm(inputs, gain_one, shift_one).astype(jnp.bfloat16)
    mixing = jnp.einsum(
        "rsd,dc->rsc", normed, weights[:, : 3 * D], preferred_element_type=jnp.float32
    )
    mixing = mixing + jnp.concatenate([bias_query, jnp.zeros_like(bias_query), bias_value])
    head_parts = mixing.astype(jnp.bfloat16).reshape(row_count, seq_tokens, 3, HEADS, HEAD_DIM)
    query_heads, key_heads, value_heads = (
        head_parts[:, :, 0],
        head_parts[:, :, 1],
        head_parts[:, :, 2],
    )
    scores = masked_scores(query_heads, key_heads, allowed)
    highest = jnp.max(scores, axis=-1, keepdims=True)
    log_total = highest + jnp.log(jnp.sum(jnp.exp(scores - highest), axis=-1, keepdims=True))
    attention = jnp.exp(scores - log_total).astype(jnp.bfloat16)
    mixed_heads = jnp.einsum(
        "rhst,rthd->rshd", attention, value_heads, preferred_element_type=jnp.float32
    )
    mixed_heads = mixed_heads.reshape(row_count, seq_tokens, D).astype(jnp.bfloat16)
    attended = (
        jnp.einsum(
            "rsd,de->rse",
            mixed_heads,
            weights[:, 3 * D : 4 * D],
            preferred_element_type=jnp.float32,
        )
        + bias_out
    )
    middle = inputs + attended
    normed_two = layer_norm(middle, gain_two, shift_two).astype(jnp.bfloat16)
    hidden = (
        jnp.einsum(
            "rsd,df->rsf",
            normed_two,
            weights[:, 4 * D : 4 * D + FF],
            preferred_element_type=jnp.float32,
        )
        + bias_expand
    )
    active = jax.nn.gelu(hidden, approximate=False).astype(jnp.bfloat16)
    shrunk = (
        jnp.einsum(
            "rsf,df->rsd", active, weights[:, 4 * D + FF :], preferred_element_type=jnp.float32
        )
        + bias_shrink
    )
    forward_kept = (
        normed,
        query_heads,
        key_heads,
        value_heads,
        log_total,
        mixed_heads,
        middle,
        normed_two,
        hidden,
        active,
    )
    return (middle + shrunk, forward_kept)


def token_sum(values_low):
    return jnp.sum(values_low.astype(jnp.float32).reshape(-1, values_low.shape[-1]), axis=0)


def block_backward(inputs, allowed, weights, vector_pieces, forward_kept, grad_out):
    (
        gain_one,
        shift_one,
        bias_query,
        bias_value,
        bias_out,
        gain_two,
        shift_two,
        bias_shrink,
        bias_expand,
    ) = vector_pieces
    (
        normed,
        query_heads,
        key_heads,
        value_heads,
        log_total,
        mixed_heads,
        middle,
        normed_two,
        hidden,
        active,
    ) = forward_kept
    row_count, seq_tokens = (inputs.shape[0], inputs.shape[1])
    grad_shrunk = grad_out.astype(jnp.bfloat16)
    grad_active = jnp.einsum(
        "rsd,df->rsf", grad_shrunk, weights[:, 4 * D + FF :], preferred_element_type=jnp.float32
    )
    _, gelu_back = jax.vjp(lambda before_gelu: jax.nn.gelu(before_gelu, approximate=False), hidden)
    grad_hidden = gelu_back(grad_active)[0].astype(jnp.bfloat16)
    grad_normed_two = jnp.einsum(
        "rsf,df->rsd",
        grad_hidden,
        weights[:, 4 * D : 4 * D + FF],
        preferred_element_type=jnp.float32,
    )
    _, norm_two_back = jax.vjp(layer_norm, middle, gain_two, shift_two)
    grad_middle, grad_gain_two, grad_shift_two = norm_two_back(grad_normed_two)
    grad_middle = grad_middle + grad_out
    grad_attended = grad_middle.astype(jnp.bfloat16)
    grad_mixed = jnp.einsum(
        "rse,de->rsd", grad_attended, weights[:, 3 * D : 4 * D], preferred_element_type=jnp.float32
    )
    grad_mixed = grad_mixed.astype(jnp.bfloat16).reshape(row_count, seq_tokens, HEADS, HEAD_DIM)
    attention = jnp.exp(masked_scores(query_heads, key_heads, allowed) - log_total)
    grad_values = jnp.einsum(
        "rhst,rshd->rthd",
        attention.astype(jnp.bfloat16),
        grad_mixed,
        preferred_element_type=jnp.float32,
    )
    grad_attention = jnp.einsum(
        "rshd,rthd->rhst", grad_mixed, value_heads, preferred_element_type=jnp.float32
    )
    grad_scores = attention * (
        grad_attention - jnp.sum(attention * grad_attention, axis=-1, keepdims=True)
    )
    grad_scores = grad_scores.astype(jnp.bfloat16)
    grad_query = (
        jnp.einsum("rhst,rthd->rshd", grad_scores, key_heads, preferred_element_type=jnp.float32)
        * SCORE_SCALE
    )
    grad_keys = (
        jnp.einsum("rhst,rshd->rthd", grad_scores, query_heads, preferred_element_type=jnp.float32)
        * SCORE_SCALE
    )
    grad_mixing = (
        jnp.stack([grad_query, grad_keys, grad_values], axis=2)
        .reshape(row_count, seq_tokens, 3 * D)
        .astype(jnp.bfloat16)
    )
    grad_normed = jnp.einsum(
        "rsc,dc->rsd", grad_mixing, weights[:, : 3 * D], preferred_element_type=jnp.float32
    )
    _, norm_one_back = jax.vjp(layer_norm, inputs, gain_one, shift_one)
    grad_inputs, grad_gain_one, grad_shift_one = norm_one_back(grad_normed)
    grad_inputs = grad_inputs + grad_middle
    vector_grad = jnp.concatenate(
        [
            grad_gain_one,
            grad_shift_one,
            token_sum(grad_mixing[..., :D]),
            token_sum(grad_mixing[..., 2 * D :]),
            token_sum(grad_attended),
            grad_gain_two,
            grad_shift_two,
            token_sum(grad_shrunk),
            token_sum(grad_hidden),
        ]
    )
    tokens = row_count * seq_tokens
    outer_terms = (
        (normed.reshape(tokens, D), grad_mixing.reshape(tokens, 3 * D)),
        (mixed_heads.reshape(tokens, D), grad_attended.reshape(tokens, D)),
        (normed_two.reshape(tokens, D), grad_hidden.reshape(tokens, FF)),
        (grad_shrunk.reshape(tokens, D), active.reshape(tokens, FF)),
    )
    return (grad_inputs, vector_grad, outer_terms)


def orthonormal(stacked):
    finished = []
    for column_id in range(stacked.shape[1]):
        vector = stacked[:, column_id]
        for earlier in finished:
            vector = vector - jnp.sum(earlier * vector, axis=-1, keepdims=True) * earlier
        vector = vector / (jnp.sqrt(jnp.sum(vector * vector, axis=-1, keepdims=True)) + NORM_FLOOR)
        finished.append(vector)
    return jnp.stack(finished, axis=1)


def rows_factor(start_part, row_block):
    return jnp.einsum("kc,dc->kd", start_part, row_block, precision=PRECISE)


def per_device(
    image_tokens,
    image_weights,
    image_vectors,
    text_tokens,
    segments,
    text_weights,
    text_vectors,
    momentum,
    vector_momentum,
    error_feedback,
    start_factors,
):
    rep_count = lax.axis_size("rep")
    device_pairs = image_tokens.shape[0]
    patches = image_tokens.shape[1]
    pair_total = device_pairs * lax.axis_size("dp") * rep_count
    own_rows = text_weights.shape[0]
    row_start = lax.axis_index("dp") * own_rows
    factor_rank = start_factors.shape[0]
    bounds = matrix_bounds()
    text_low, frozen = (
        lax.all_gather(text_weights.astype(jnp.bfloat16), "dp", axis=0, tiled=True),
        lax.all_gather(image_weights, "dp", axis=0, tiled=True),
    )
    full_mask = jnp.zeros((device_pairs, patches, patches), jnp.int32) == 0
    image_out, _ = block_forward(
        image_tokens.astype(jnp.float32), full_mask, frozen, vector_parts(image_vectors)
    )
    image_emb = unit_rows(jnp.mean(image_out, axis=1)).astype(jnp.bfloat16)
    text_float = text_tokens.astype(jnp.float32)
    allowed = segments[:, :, None] == segments[:, None, :]
    vector_pieces = vector_parts(text_vectors)
    text_output, forward_kept = block_forward(text_float, allowed, text_low, vector_pieces)
    caption_marks = (
        segments[:, None, :] == jnp.arange(PER_ROW, dtype=jnp.int32)[None, :, None]
    ).astype(jnp.float32)
    counts = jnp.sum(caption_marks, axis=-1, keepdims=True)
    pooled = (
        jnp.einsum("rks,rsd->rkd", caption_marks, text_output, precision=PRECISE) / counts
    ).reshape(-1, D)
    text_norm, embed_back = jax.vjp(unit_rows, pooled)
    text_emb = text_norm.astype(jnp.bfloat16)
    image_all, text_all = (
        lax.all_gather(image_emb, ("dp", "rep"), axis=0, tiled=True),
        lax.all_gather(text_emb, ("dp", "rep"), axis=0, tiled=True),
    )
    offset = lax.axis_index(("dp", "rep")) * device_pairs
    diagonal_pick = (
        jnp.arange(pair_total, dtype=jnp.int32)[None, :]
        == offset + jnp.arange(device_pairs, dtype=jnp.int32)[:, None]
    ).astype(jnp.float32)
    image_logits = LOGIT_SCALE * jnp.einsum(
        "pd,bd->pb", image_emb, text_all, preferred_element_type=jnp.float32
    )
    text_logits = LOGIT_SCALE * jnp.einsum(
        "pd,bd->pb", text_emb, image_all, preferred_element_type=jnp.float32
    )
    image_log_total = row_log_total(image_logits)
    text_log_total = row_log_total(text_logits)
    loss_part = (
        jnp.sum(image_log_total - jnp.sum(diagonal_pick * image_logits, axis=1))
        + jnp.sum(text_log_total - jnp.sum(diagonal_pick * text_logits, axis=1))
    ) / (2.0 * pair_total)
    text_soft = ((jnp.exp(text_logits - text_log_total[:, None]) - diagonal_pick) * 0.5).astype(
        jnp.bfloat16
    )
    grad_text = LOGIT_SCALE * jnp.einsum(
        "pb,bd->pd", text_soft, image_all, preferred_element_type=jnp.float32
    )
    log_totals = lax.all_gather(image_log_total, ("dp", "rep"), axis=0, tiled=True)
    column_soft = ((jnp.exp(text_logits - log_totals[None, :]) - diagonal_pick) * 0.5).astype(
        jnp.bfloat16
    )
    grad_text = grad_text + LOGIT_SCALE * jnp.einsum(
        "pb,bd->pd", column_soft, image_all, preferred_element_type=jnp.float32
    )
    grad_pooled = embed_back(grad_text)[0].reshape(-1, PER_ROW, D) / counts
    grad_out = jnp.einsum("rks,rkd->rsd", caption_marks, grad_pooled, precision=PRECISE)
    grad_inputs, vector_grad, outer_terms = block_backward(
        text_float, allowed, text_low, vector_pieces, forward_kept, grad_out
    )
    blocks = [
        jnp.einsum("tc,tk->ck", left_side, right_side, preferred_element_type=jnp.float32)
        for left_side, right_side in outer_terms
    ]
    grad_rows = lax.psum_scatter(
        jnp.concatenate(blocks, axis=1), "dp", scatter_dimension=0, tiled=True
    )
    feedback_rows = error_feedback[0]
    worker_rows = grad_rows + feedback_rows
    factor_rows = jnp.concatenate(
        [
            rows_factor(start_factors[:, first_col:after_col], worker_rows[:, first_col:after_col])
            for first_col, after_col in bounds
        ],
        axis=0,
    )
    gathered_rows = lax.all_gather(factor_rows, "dp", axis=1, tiled=True)
    factor = lax.psum(gathered_rows.astype(jnp.bfloat16), "rep").astype(jnp.float32)
    vector_total, loss_total = lax.psum((vector_grad, loss_part), ("dp", "rep"))
    left_basis = orthonormal(factor.reshape(4, factor_rank, D)).reshape(4 * factor_rank, D)
    basis_rows = lax.dynamic_slice_in_dim(left_basis, row_start, own_rows, 1)
    right_part = jnp.concatenate(
        [
            jnp.einsum(
                "kd,dc->kc",
                basis_rows[matrix_id * factor_rank : (matrix_id + 1) * factor_rank],
                worker_rows[:, bounds[matrix_id][0] : bounds[matrix_id][1]],
                precision=PRECISE,
            )
            for matrix_id in range(4)
        ],
        axis=1,
    )
    new_right = lax.psum(right_part, ("dp", "rep"))
    approximation = jnp.concatenate(
        [
            jnp.einsum(
                "kd,kc->dc",
                basis_rows[matrix_id * factor_rank : (matrix_id + 1) * factor_rank],
                new_right[:, bounds[matrix_id][0] : bounds[matrix_id][1]],
                precision=PRECISE,
            )
            for matrix_id in range(4)
        ],
        axis=1,
    )
    new_feedback = (worker_rows - approximation / rep_count)[None]
    new_momentum = MOMENTUM_DECAY * momentum + approximation
    new_weights = text_weights - STEP_RATE * new_momentum
    new_vector_momentum = MOMENTUM_DECAY * vector_momentum + vector_total
    new_vectors = text_vectors - STEP_RATE * new_vector_momentum
    return (
        loss_total,
        text_output,
        grad_inputs,
        new_weights,
        new_momentum,
        new_feedback,
        new_vectors,
        new_vector_momentum,
        left_basis,
        new_right,
    )


def solution(mesh):
    placed = (
        P(("dp", "rep"), None, None),
        P("dp", None),
        P(),
        P(("dp", "rep"), None, None),
        P(("dp", "rep"), None),
        P("dp", None),
        P(),
        P("dp", None),
        P(),
        P("rep", "dp", None),
        P(),
    )
    return jax.shard_map(
        per_device,
        mesh=mesh,
        in_specs=placed,
        out_specs=(
            P(),
            P(("dp", "rep"), None, None),
            P(("dp", "rep"), None, None),
            P("dp", None),
            P("dp", None),
            P("rep", "dp", None),
            P(),
            P(),
            P(),
            P(),
        ),
        check_vma=False,
    )
```

profile of v0, /device:TPU:8, one launch (start us, length us, event | category | flops | bytes accessed | tf_op | source)
XLA Modules:
  0.0 1259.0 jit_solution(4314769996404762950)
XLA Ops:
  8.0 3.5 convert_element_type.126
  14.4 190.8 %all-gather.4.cloned.1.call-done = bf16[768,9216]{1,0:T(8,128)(2,1)} async-done(((bf16[96,9216]{1,0:T(8,128)(2,1)}), bf16[768,9216]{1,0:T(8,128)(2,1)}) %all-gather.4.cloned.1.call-update) | async-done | bytes 14155792 | tf_op jit(solution)/shard_map/all_gather | solution.py:270
  205.2 5.4 fusion.11
  210.5 5.9 reshape.907
  216.4 4.0 fusion.234
  223.5 1.5 reshape.906
  225.0 2.1 fusion.238
  227.4 6.5 fusion.72
  233.9 17.2 %fusion.76 = f32[8,768]{1,0:T(8,128)S(1)} fusion(f32[8,50,768]{2,1,0:T(8,128)S(1)} %get-tuple-element.130, bf16[768,9216]{1,0:T(8,128)(2,1)} %all-gather.4.cloned.1.call-done, f32[8,50,3072]{2,1,0:T(8,128)S(1)} %get-tuple-element.131, f32[3072]{0:T(1024)S(1)} %slice.199, u8[50,3072]{1,0:T(8,128)(4,1)S(1)} %get-tuple-element.11, ...), kind=kOutput, calls=%fused_computation.137 | convolution fusion | flops 1975597056 | bytes 11209728 | tf_op jit(solution)/shard_map/rsf,df->rsd/dot_general | solution.py:107
  251.9 149.9 %all-gather.6.cloned.1.call-done = bf16[768,9216]{1,0:T(8,128)(2,1)} async-done(((bf16[96,9216]{1,0:T(8,128)(2,1)}), bf16[768,9216]{1,0:T(8,128)(2,1)}) %all-gather.6.cloned.1.call-update) | async-done | bytes 14155792 | tf_op jit(solution)/shard_map/all_gather | solution.py:269
  401.8 2.7 fusion.12
  404.5 1.0 reshape.882
  405.5 1.1 fusion.235
  407.0 1.4 fusion.239
  408.9 1.7 fusion.240
  410.8 3.7 fusion.130
  414.7 1.1 copy-done.10
  415.8 4.4 multiply_convert_fusion
  420.2 4.3 fusion.84
  425.2 35.1 %all_gather.20 = bf16[256,768]{1,0:T(8,128)(2,1)S(1)} all-gather(bf16[8,768]{1,0:T(8,128)(2,1)S(1)} %multiply_convert_fusion.2), channel_id=1, replica_groups=mesh['dp'=8,'rep'=4] {'dp','rep'}, dimensions={0}, use_global_device_ids=true | all-gather | bytes 405504 | tf_op jit(solution)/shard_map/all_gather | solution.py:292
  460.3 37.8 %all_gather.21 = bf16[256,768]{1,0:T(8,128)(2,1)S(1)} all-gather(bf16[8,768]{1,0:T(8,128)(2,1)S(1)} %copy-done.23), channel_id=1, replica_groups=mesh['dp'=8,'rep'=4] {'dp','rep'}, dimensions={0}, use_global_device_ids=true | all-gather | bytes 405504 | tf_op jit(solution)/shard_map/all_gather | solution.py:291
  500.7 44.9 %all-reduce = f32[256]{0:T(256)S(1)} all-reduce(f32[256]{0:T(256)S(1)} %get-tuple-element.123), channel_id=1, replica_groups=mesh['dp'=8,'rep'=4] {'dp','rep'}, use_global_device_ids=true, to_apply=%add | all-reduce | flops 256 | bytes 2048
  546.5 5.3 convert_reduce_fusion.1
  551.8 5.0 multiply_reduce_fusion.3
  557.8 1.8 convolution_convert_fusion.3
  561.8 5.0 convolution_bitcast_fusion
  566.9 5.1 convolution_bitcast_fusion.1
  572.8 2.0 copy.270
  574.8 2.2 convert_element_type.144
  577.0 4.1 convolution_bitcast_fusion.2
  581.1 19.5 %pad_maximum_fusion = f32[768,9216]{1,0:T(8,128)} fusion(f32[768,3072]{1,0:T(8,128)} %convolution_bitcast_fusion, f32[768,3072]{1,0:T(8,128)} %convolution_bitcast_fusion.1, f32[768,768]{1,0:T(8,128)S(1)} %convolution_bitcast_fusion.3, f32[768,2304]{1,0:T(8,128)} %convolution_bitcast_fusion.2), kind=kLoop, calls=%fused_computation | loop fusion | flops 21233664 | bytes 56623104 | tf_op jit(solution)/shard_map/concatenate | solution.py:334
  602.2 3.4 fusion.230
  607.2 45.5 %all-reduce.1 = (f32[]{:T(128)}, f32[9216]{0:T(1024)}) all-reduce(f32[]{:T(128)S(6)} %div.223, f32[9216]{0:T(1024)S(1)} %constant_dynamic-update-slice_fusion.9), channel_id=1, replica_groups=mesh['dp'=8,'rep'=4] {'dp','rep'}, use_global_device_ids=true, to_apply=%region_24.25 | all-reduce | flops 9217 | bytes 73736 | tf_op jit(solution)/shard_map/psum | solution.py:347
  652.7 395.9 %reduce-scatter.2.cloned.1.call-done = f32[96,9216]{1,0:T(8,128)} async-done(((f32[768,9216]{1,0:T(8,128)}), f32[96,9216]{1,0:T(8,128)}) %reduce-scatter.2.cloned.1.call-update) | async-done | bytes 3538960 | tf_op jit(solution)/shard_map/reduce_scatter | solution.py:333
  1048.6 3.5 bitcast_add_fusion
  1052.1 1.0 fusion.96
  1053.1 1.0 fusion.93
  1055.3 29.7 %all-gather = bf16[8,96,32]{1,2,0:T(8,128)(2,1)S(1)} all-gather(bf16[1,96,32]{1,2,0:T(8,128)(2,1)S(1)} %maximum_bitcast_fusion), channel_id=1, replica_groups=mesh['dp'=8,'rep'=4] {'dp'}, dimensions={0}, use_global_device_ids=true | all-gather | bytes 55296 | tf_op jit(solution)/shard_map/all_gather | solution.py:345
  1085.7 1.6 reshape.893
  1087.3 1.4 copy.274
  1088.7 11.6 psum.29
  1108.3 1.4 multiply_subtract_fusion.1
  1109.8 128.2 %all-reduce.4.cloned.1.call-done = f32[8,9216]{1,0:T(8,128)} async-done(((f32[8,9216]{1,0:T(8,128)}), f32[8,9216]{1,0:T(8,128)}) %all-reduce.4.cloned.1.call-update) | async-done | bytes 294928 | tf_op jit(solution)/shard_map/psum | solution.py:362
  1238.0 2.2 fusion.138
  1240.2 2.1 fusion.140
  1242.3 1.3 fusion.151
  1243.6 1.9 fusion.146
  1245.5 6.1 multiply_subtract_fusion
  (239 shorter events, 28.8 us)
Async XLA Ops:
  7.2 198.0 %all-gather.4.cloned.1.call-start = ((), (), s32[]{:S(2)}) async-start(), calls=%async_computation.1 | async-start | bytes 15925248 | tf_op jit(solution)/shard_map/all_gather | solution.py:270
  7.9 3.7 copy-start.28
  7.9 4.2 copy-start.36
  7.9 4.9 copy-start.18
  7.9 5.5 copy-start.1
  8.0 5.8 copy-start.6
  8.0 393.8 %all-gather.6.cloned.1.call-start = ((), (), s32[]{:S(2)}) async-start(), calls=%async_computation.2 | async-start | bytes 15925248 | tf_op jit(solution)/shard_map/all_gather | solution.py:269
  11.5 1037.0 %reduce-scatter.2.cloned.1.call-start = ((), (), s32[]{:S(2)}) async-start(), calls=%async_computation.3 | async-start | bytes 31850496 | tf_op jit(solution)/shard_map/reduce_scatter | solution.py:333
  13.4 388.4 %copy-start.16 = (f32[768]{0:T(1024)}, f32[768]{0:T(1024)S(1)}, u32[]{:S(2)}) copy-start(f32[768]{0:T(1024)S(1)} %get-tuple-element.112) | copy-start | bytes 9220
  13.4 388.4 %copy-start.24 = (f32[768]{0:T(1024)}, f32[768]{0:T(1024)S(1)}, u32[]{:S(2)}) copy-start(f32[768]{0:T(1024)S(1)} %get-tuple-element.111) | copy-start | bytes 9220
  13.5 388.2 %copy-start.29 = (f32[2,64]{1,0:T(2,128)}, f32[2,64]{1,0:T(2,128)S(1)}, u32[]{:S(2)}) copy-start(f32[2,64]{1,0:T(2,128)S(1)} %broadcast_multiply_fusion.3) | copy-start | bytes 1540
  13.8 196.8 %copy-start.46 = (f32[2,64]{1,0:T(2,128)}, f32[2,64]{1,0:T(2,128)S(1)}, u32[]{:S(2)}) copy-start(f32[2,64]{1,0:T(2,128)S(1)} %fusion.124) | copy-start | bytes 1540
  14.3 387.5 %copy-start.31 = (f32[2,64]{1,0:T(2,128)}, f32[2,64]{1,0:T(2,128)S(1)}, u32[]{:S(2)}) copy-start(f32[2,64]{1,0:T(2,128)S(1)} %fusion.189) | copy-start | bytes 1540
  408.4 2.5 slice-start
  410.6 4.0 copy-start.33
  410.8 3.8 copy-start.48
  410.8 3.8 copy-start.38
  414.6 5.6 copy-start.50
  420.2 4.4 copy-start.4
  420.2 4.4 copy-start.37
  420.2 4.4 copy-start.43
  420.2 40.1 %copy-start.23 = (bf16[8,768]{1,0:T(8,128)(2,1)S(1)}, bf16[8,768]{1,0:T(8,128)(2,1)}, u32[]{:S(2)}) copy-start(bf16[8,768]{1,0:T(8,128)(2,1)} %multiply_convert_fusion.3) | copy-start | bytes 36868
  420.2 78.6 %copy-start.53 = (s32[8]{0:T(128)S(1)}, s32[8]{0:T(128)}, u32[]{:S(2)}) copy-start(s32[8]{0:T(128)} %iota_add_fusion) | copy-start | bytes 100
  424.6 121.4 %copy-start.14 = (f32[2,64,768]{2,1,0:T(8,128)}, f32[2,64,768]{2,1,0:T(8,128)S(1)}, u32[]{:S(2)}) copy-start(f32[2,64,768]{2,1,0:T(8,128)S(1)} %fusion.84) | copy-start | bytes 1179652
  546.4 5.3 copy-start.21
  546.4 5.3 copy-start.34
  546.5 5.3 copy-start.39
  551.8 5.0 copy-start.12
  551.8 5.0 copy-start.49
  561.8 5.1 copy-start.13
  561.8 5.1 copy-start.22
  561.8 5.1 copy-start.27
  561.8 5.1 copy-start.35
  561.8 5.1 copy-start.40
  572.8 4.2 copy-start.17
  572.8 4.2 copy-start.25
  572.8 4.2 copy-start.30
  572.8 4.2 copy-start.32
  600.6 637.4 %all-reduce.4.cloned.1.call-start = ((), (), s32[]{:S(2)}) async-start(), calls=%async_computation.4 | async-start | bytes 589824 | tf_op jit(solution)/shard_map/psum | solution.py:362
  602.2 3.5 copy-start.47
  602.2 3.9 copy-start.41
  602.2 3.9 copy-start.52
  602.2 4.0 copy-start.51
  602.2 4.0 copy-start.3
  602.2 4.0 copy-start.45
  1048.6 3.5 copy-start.15
  1238.0 7.5 copy-start
  1245.5 6.1 copy-start.11
  (11 other events, 16.4 us)
Sparse Core Ops, SparseCore 0:
  10.2 194.9 all-gather.3
  207.9 193.7 all-gather.5
  600.7 447.8 reduce-scatter.1
  1108.4 129.5 all-reduce.3
where the time goes:
time: 1270 us; the launch traced here: 1260 us
  waiting for transfers between devices  865 us (68%)
  blocking collectives  205 us (16%)
  matrix products  93.6 us (7%)
  other arithmetic  53.1 us (4%)
  local copies, waits for them, and re-layouts  25.4 us (2%)
  between operations  16.5 us (1%)
    reduce_scatter x1, waiting for transfers between devices, per_device(): lax.psum_scatter(jnp.concatenate(blocks, axis=1), 'dp', scatter_dimension...  396 us
    all_gather x1, waiting for transfers between devices, per_device(): lax.all_gather(image_weights, 'dp', axis=0, tiled=True)  191 us
    all_gather x1, waiting for transfers between devices, per_device(): lax.all_gather(text_weights.astype(jnp.bfloat16), 'dp', axis=0, tiled=True)  150 us
    psum x1, waiting for transfers between devices, per_device(): new_right = lax.psum(right_part, ('dp', 'rep'))  128 us
    psum x1, blocking collectives, per_device(): vector_total, loss_total = lax.psum((vector_grad, loss_part), ('dp', 'rep'))  45.5 us
    unnamed x1, blocking collectives  44.9 us
    all_gather x1, blocking collectives, per_device(): lax.all_gather(image_emb, ('dp', 'rep'), axis=0, tiled=True)  37.8 us
    all_gather x1, blocking collectives, per_device(): lax.all_gather(text_emb, ('dp', 'rep'), axis=0, tiled=True)  35.1 us
  transfers between devices with their start and end apart: 4, of which 4 were waited for; matrix products, arithmetic and copies ran while one was open for 5% of the time, Pallas kernels for 0%

commit v1 on v0

--- a/solution.py
+++ b/solution.py
@@ -1,3 +1,4 @@
+import functools
 import jax
 import jax.numpy as jnp
 from jax import lax
@@ -16,6 +17,34 @@
 STEP_RATE = 0.08
 NORM_FLOOR = 1e-08
 MASKED = -1e30
+
+
+def switch_row(z_in, link_axis):
+    row_out = jax.lax.axis_size(link_axis)
+    h_now, vec_out, field_out = (row_out, jax.lax.axis_index(link_axis), z_in.shape[0])
+    nodes = [c * h_now if m == 0 else c for m, c in enumerate(z_in.shape)]
+    r_now = lax.dynamic_update_slice_in_dim(
+        jnp.zeros(nodes, z_in.dtype), z_in, vec_out * field_out, axis=0
+    )
+    mixed_arr = a_next = z_in
+    for u in range(1, h_now // 2 + 1):
+        mixed_arr = jax.lax.ppermute(
+            mixed_arr, axis_name=link_axis, perm=[(m, (m + 1) % h_now) for m in range(h_now)]
+        )
+        r_now = lax.dynamic_update_slice_in_dim(
+            r_now, mixed_arr, (vec_out - u) % h_now * field_out, axis=0
+        )
+        if 2 * u < h_now:
+            a_next = jax.lax.ppermute(
+                a_next, link_axis, perm=[(m, (m - 1) % h_now) for m in range(h_now)]
+            )
+            r_now = lax.dynamic_update_slice_in_dim(
+                r_now, a_next, (vec_out + u) % h_now * field_out, axis=0
+            )
+    return r_now
+
+
+work_the_threads = functools.partial(switch_row, link_axis="dp")
 
 
 def layer_norm(values, layer_gain, layer_shift):
@@ -266,7 +295,7 @@
     factor_rank = start_factors.shape[0]
     bounds = matrix_bounds()
     text_low, frozen = (
-        lax.all_gather(text_weights.astype(jnp.bfloat16), "dp", axis=0, tiled=True),
+        work_the_threads(text_weights.astype(jnp.bfloat16)),
         lax.all_gather(image_weights, "dp", axis=0, tiled=True),
     )
     full_mask = jnp.zeros((device_pairs, patches, patches), jnp.int32) == 0

time: 1270 us -> 1330 us (1.047)
  local copies, waits for them, and re-layouts: 25.4 us -> 47.8 us
  waiting for transfers between devices: 865 us -> 885 us
    ppermute x0 -> x7, waiting for transfers between devices: none -> 360 us  [the longest x4 332 us: switch_row(): jax.lax.ppermute(mixed_arr, axis_name=link_axis, perm=[(m, (m + 1) % h_no...]
    all_gather x1, waiting for transfers between devices: 191 us -> 0.01 us  [per_device(): lax.all_gather(image_weights, 'dp', axis=0, tiled=True)]
    all_gather x1 -> x0, waiting for transfers between devices: 150 us -> none  [per_device(): lax.all_gather(text_weights.astype(jnp.bfloat16), 'dp', axis=0, tiled=True)]
  transfers between devices with their start and end apart: 4 -> 10, of which waited for: 4 -> 8; matrix products, arithmetic and copies ran while one was open for 5% -> 4% of each run, Pallas kernels for 0% -> 0%
where the time goes in v1:
time: 1330 us; the launch traced here: 1320 us
  waiting for transfers between devices  885 us (67%)
  blocking collectives  206 us (15%)
  matrix products  93.9 us (7%)
  other arithmetic  56.9 us (4%)
  local copies, waits for them, and re-layouts  47.8 us (4%)
  between operations  16.8 us (1%)
    reduce_scatter x1, waiting for transfers between devices, per_device(): lax.psum_scatter(jnp.concatenate(blocks, axis=1), 'dp', scatter_dimension...  395 us
    ppermute x4, waiting for transfers between devices, switch_row(): jax.lax.ppermute(mixed_arr, axis_name=link_axis, perm=[(m, (m + 1) % h_no...  332 us
    psum x1, waiting for transfers between devices, per_device(): new_right = lax.psum(right_part, ('dp', 'rep'))  128 us
    psum x1, blocking collectives, per_device(): vector_total, loss_total = lax.psum((vector_grad, loss_part), ('dp', 'rep'))  45.6 us
    unnamed x1, blocking collectives  44.7 us
    all_gather x1, blocking collectives, per_device(): lax.all_gather(image_emb, ('dp', 'rep'), axis=0, tiled=True)  37.7 us
    all_gather x1, blocking collectives, per_device(): lax.all_gather(text_emb, ('dp', 'rep'), axis=0, tiled=True)  36.5 us
    all_gather x1, blocking collectives, per_device(): gathered_rows = lax.all_gather(factor_rows, 'dp', axis=1, tiled=True)  29.7 us
  transfers between devices with their start and end apart: 10, of which 8 were waited for; matrix products, arithmetic and copies ran while one was open for 4% of the time, Pallas kernels for 0%

profile of v1, /device:TPU:8, one launch (start us, length us, event | category | flops | bytes accessed | tf_op | source)
XLA Modules:
  0.0 1317.1 jit_solution(4429269591691125172)
XLA Ops:
  8.0 6.7 broadcast_in_dim.34
  14.7 2.2 constant_dynamic-update-slice_fusion.24
  16.9 1.5 collective-permute-start
  32.0 81.5 %collective-permute-done = bf16[96,9216]{1,0:T(8,128)(2,1)S(1)} collective-permute-done((bf16[96,9216]{1,0:T(8,128)(2,1)}, bf16[96,9216]{1,0:T(8,128)(2,1)S(1)}, u32[]{:S(2)}, u32[]{:S(2)}) %collective-permute-start) | collective-permute-done | bytes 1769504 | tf_op jit(solution)/shard_map/ppermute | solution.py:31
  113.5 2.4 collective-permute-start.2
  119.1 105.3 %collective-permute-done.2 = bf16[96,9216]{1,0:T(8,128)(2,1)S(1)} collective-permute-done((bf16[96,9216]{1,0:T(8,128)(2,1)S(1)}, bf16[96,9216]{1,0:T(8,128)(2,1)S(1)}, u32[]{:S(2)}, u32[]{:S(2)}) %collective-permute-start.2) | collective-permute-done | bytes 1769504 | tf_op jit(solution)/shard_map/ppermute | solution.py:31
  224.3 2.5 collective-permute-start.4
  226.8 17.9 %collective-permute-done.3 = bf16[96,9216]{1,0:T(8,128)(2,1)S(1)} collective-permute-done((bf16[96,9216]{1,0:T(8,128)(2,1)S(1)}, bf16[96,9216]{1,0:T(8,128)(2,1)S(1)}, u32[]{:S(2)}, u32[]{:S(2)}) %collective-permute-start.3) | collective-permute-done | bytes 1769504 | tf_op jit(solution)/shard_map/ppermute | solution.py:38
  247.5 93.2 %collective-permute-done.4 = bf16[96,9216]{1,0:T(8,128)(2,1)S(1)} collective-permute-done((bf16[96,9216]{1,0:T(8,128)(2,1)S(1)}, bf16[96,9216]{1,0:T(8,128)(2,1)S(1)}, u32[]{:S(2)}, u32[]{:S(2)}) %collective-permute-start.4) | collective-permute-done | bytes 1769504 | tf_op jit(solution)/shard_map/ppermute | solution.py:31
  340.7 2.5 collective-permute-start.6
  344.6 10.2 collective-permute-done.5
  356.1 52.3 %collective-permute-done.6 = bf16[96,9216]{1,0:T(8,128)(2,1)S(1)} collective-permute-done((bf16[96,9216]{1,0:T(8,128)(2,1)S(1)}, bf16[96,9216]{1,0:T(8,128)(2,1)S(1)}, u32[]{:S(2)}, u32[]{:S(2)}) %collective-permute-start.6) | collective-permute-done | bytes 1769504 | tf_op jit(solution)/shard_map/ppermute | solution.py:31
  409.8 2.7 fusion.12
  416.9 1.7 fusion.240
  418.9 3.8 fusion.130
  423.8 4.4 multiply_convert_fusion
  428.3 4.3 fusion.84
  433.5 36.5 %all_gather.16 = bf16[256,768]{1,0:T(8,128)(2,1)S(1)} all-gather(bf16[8,768]{1,0:T(8,128)(2,1)S(1)} %multiply_convert_fusion.2), channel_id=1, replica_groups=mesh['dp'=8,'rep'=4] {'dp','rep'}, dimensions={0}, use_global_device_ids=true | all-gather | bytes 405504 | tf_op jit(solution)/shard_map/all_gather | solution.py:321
  470.0 5.5 fusion.11
  475.5 5.9 reshape.907
  481.4 3.4 fusion.234
  489.0 3.3 reshape.906
  492.5 2.3 fusion.238
  495.1 6.4 fusion.72
  501.6 17.2 %fusion.76 = f32[8,768]{1,0:T(8,128)S(1)} fusion(f32[8,50,768]{2,1,0:T(8,128)S(1)} %get-tuple-element.132, bf16[768,9216]{1,0:T(8,128)(2,1)} %all-gather.3.cloned.1.call-done, f32[8,50,3072]{2,1,0:T(8,128)S(1)} %get-tuple-element.133, f32[3072]{0:T(1024)S(1)} %copy-done.44, u8[50,3072]{1,0:T(8,128)(4,1)S(1)} %get-tuple-element.11, ...), kind=kOutput, calls=%fused_computation.137 | convolution fusion | flops 1975597056 | bytes 11209728 | tf_op jit(solution)/shard_map/rsf,df->rsd/dot_general | solution.py:136
  518.9 37.7 %all_gather.17 = bf16[256,768]{1,0:T(8,128)(2,1)S(1)} all-gather(bf16[8,768]{1,0:T(8,128)(2,1)S(1)} %multiply_convert_fusion.3), channel_id=1, replica_groups=mesh['dp'=8,'rep'=4] {'dp','rep'}, dimensions={0}, use_global_device_ids=true | all-gather | bytes 405504 | tf_op jit(solution)/shard_map/all_gather | solution.py:320
  559.2 44.7 %all-reduce = f32[256]{0:T(256)S(1)} all-reduce(f32[256]{0:T(256)S(1)} %get-tuple-element.125), channel_id=1, replica_groups=mesh['dp'=8,'rep'=4] {'dp','rep'}, use_global_device_ids=true, to_apply=%add | all-reduce | flops 256 | bytes 2048
  604.8 5.3 convert_reduce_fusion.1
  610.1 5.0 multiply_reduce_fusion.3
  616.1 1.8 convolution_convert_fusion.3
  620.1 5.0 convolution_bitcast_fusion
  625.2 5.1 convolution_bitcast_fusion.1
  631.2 2.0 copy.270
  633.1 2.2 convert_element_type.144
  635.3 4.1 convolution_bitcast_fusion.2
  639.4 19.5 %pad_maximum_fusion = f32[768,9216]{1,0:T(8,128)} fusion(f32[768,3072]{1,0:T(8,128)} %convolution_bitcast_fusion, f32[768,3072]{1,0:T(8,128)} %convolution_bitcast_fusion.1, f32[768,768]{1,0:T(8,128)S(1)} %convolution_bitcast_fusion.3, f32[768,2304]{1,0:T(8,128)} %convolution_bitcast_fusion.2), kind=kLoop, calls=%fused_computation | loop fusion | flops 21233664 | bytes 56623104 | tf_op jit(solution)/shard_map/concatenate | solution.py:363
  660.5 3.4 fusion.230
  665.5 45.6 %all-reduce.1 = (f32[]{:T(128)}, f32[9216]{0:T(1024)}) all-reduce(f32[]{:T(128)S(6)} %div.223, f32[9216]{0:T(1024)S(1)} %constant_dynamic-update-slice_fusion.9), channel_id=1, replica_groups=mesh['dp'=8,'rep'=4] {'dp','rep'}, use_global_device_ids=true, to_apply=%region_24.25 | all-reduce | flops 9217 | bytes 73736 | tf_op jit(solution)/shard_map/psum | solution.py:376
  711.1 395.3 %reduce-scatter.2.cloned.1.call-done = f32[96,9216]{1,0:T(8,128)} async-done(((f32[768,9216]{1,0:T(8,128)}), f32[96,9216]{1,0:T(8,128)}) %reduce-scatter.2.cloned.1.call-update) | async-done | bytes 3538960 | tf_op jit(solution)/shard_map/reduce_scatter | solution.py:362
  1106.4 3.5 bitcast_add_fusion
  1113.2 29.7 %all-gather = bf16[8,96,32]{1,2,0:T(8,128)(2,1)S(1)} all-gather(bf16[1,96,32]{1,2,0:T(8,128)(2,1)S(1)} %maximum_bitcast_fusion), channel_id=1, replica_groups=mesh['dp'=8,'rep'=4] {'dp'}, dimensions={0}, use_global_device_ids=true | all-gather | bytes 55296 | tf_op jit(solution)/shard_map/all_gather | solution.py:374
  1143.5 1.6 reshape.893
  1146.5 11.6 psum.29
  1167.6 128.2 %all-reduce.4.cloned.1.call-done = f32[8,9216]{1,0:T(8,128)} async-done(((f32[8,9216]{1,0:T(8,128)}), f32[8,9216]{1,0:T(8,128)}) %all-reduce.4.cloned.1.call-update) | async-done | bytes 294928 | tf_op jit(solution)/shard_map/psum | solution.py:391
  1295.8 2.2 fusion.138
  1298.0 2.1 fusion.140
  1301.4 1.9 fusion.146
  1303.3 6.1 multiply_subtract_fusion
  (280 shorter events, 61.2 us)
Async XLA Ops:
  7.2 462.8 %all-gather.3.cloned.1.call-start = ((), (), s32[]{:S(2)}) async-start(), calls=%async_computation.1 | async-start | bytes 15925248 | tf_op jit(solution)/shard_map/all_gather | solution.py:299
  7.9 1098.5 %reduce-scatter.2.cloned.1.call-start = ((), (), s32[]{:S(2)}) async-start(), calls=%async_computation.2 | async-start | bytes 31850496 | tf_op jit(solution)/shard_map/reduce_scatter | solution.py:362
  8.0 6.7 copy-start
  14.7 6.5 copy-start.34
  16.9 96.6 %collective-permute-start = (bf16[96,9216]{1,0:T(8,128)(2,1)}, bf16[96,9216]{1,0:T(8,128)(2,1)S(1)}, u32[]{:S(2)}, u32[]{:S(2)}) collective-permute-start(bf16[96,9216]{1,0:T(8,128)(2,1)} %get-tuple-element.97), channel_id=1, source_target_pairs={{0,4},{4,8},{8,12},{12,16},{16,20},{20,24},{24,28},{28,0},{1,5},{5... | collective-permute-start | bytes 5308424 | tf_op jit(solution)/shard_map/ppermute | solution.py:31
  18.4 97.4 %collective-permute-start.1 = (bf16[96,9216]{1,0:T(8,128)(2,1)}, bf16[96,9216]{1,0:T(8,128)(2,1)S(1)}, u32[]{:S(2)}, u32[]{:S(2)}) collective-permute-start(bf16[96,9216]{1,0:T(8,128)(2,1)} %get-tuple-element.97), channel_id=1, source_target_pairs={{0,28},{4,0},{8,4},{12,8},{16,12},{20,16},{24,20},{28,24},{1,29},{... | collective-permute-start | bytes 5308424 | tf_op jit(solution)/shard_map/ppermute | solution.py:38
  24.7 385.1 %copy-start.17 = (f32[768]{0:T(1024)}, f32[768]{0:T(1024)S(1)}, u32[]{:S(2)}) copy-start(f32[768]{0:T(1024)S(1)} %get-tuple-element.114) | copy-start | bytes 9220
  24.7 385.1 %copy-start.23 = (f32[768]{0:T(1024)}, f32[768]{0:T(1024)S(1)}, u32[]{:S(2)}) copy-start(f32[768]{0:T(1024)S(1)} %get-tuple-element.113) | copy-start | bytes 9220
  26.9 382.9 %copy-start.27 = (f32[2,64]{1,0:T(2,128)}, f32[2,64]{1,0:T(2,128)S(1)}, u32[]{:S(2)}) copy-start(f32[2,64]{1,0:T(2,128)S(1)} %broadcast_multiply_fusion.3) | copy-start | bytes 1540
  28.0 88.4 %copy-start.50 = (f32[2,64]{1,0:T(2,128)}, f32[2,64]{1,0:T(2,128)S(1)}, u32[]{:S(2)}) copy-start(f32[2,64]{1,0:T(2,128)S(1)} %fusion.124) | copy-start | bytes 1540
  29.3 86.6 %copy-start.40 = (f32[8,50]{1,0:T(8,128)}, f32[8,50]{1,0:T(8,128)S(1)}, u32[]{:S(2)}) copy-start(f32[8,50]{1,0:T(8,128)S(1)} %broadcast_multiply_fusion.1) | copy-start | bytes 4804
  30.7 379.1 %copy-start.29 = (f32[2,64]{1,0:T(2,128)}, f32[2,64]{1,0:T(2,128)S(1)}, u32[]{:S(2)}) copy-start(f32[2,64]{1,0:T(2,128)S(1)} %fusion.191) | copy-start | bytes 1540
  113.5 110.9 %collective-permute-start.2 = (bf16[96,9216]{1,0:T(8,128)(2,1)S(1)}, bf16[96,9216]{1,0:T(8,128)(2,1)S(1)}, u32[]{:S(2)}, u32[]{:S(2)}) collective-permute-start(bf16[96,9216]{1,0:T(8,128)(2,1)S(1)} %collective-permute-done), channel_id=1, source_target_pairs={{0,4},{4,8},{8,12},{12,16},{16,20},{20,24},{24,28},{28,0},{1,5},{5... | collective-permute-start | bytes 5308424 | tf_op jit(solution)/shard_map/ppermute | solution.py:31
  115.9 128.9 %collective-permute-start.3 = (bf16[96,9216]{1,0:T(8,128)(2,1)S(1)}, bf16[96,9216]{1,0:T(8,128)(2,1)S(1)}, u32[]{:S(2)}, u32[]{:S(2)}) collective-permute-start(bf16[96,9216]{1,0:T(8,128)(2,1)S(1)} %collective-permute-done.1), channel_id=1, source_target_pairs={{0,28},{4,0},{8,4},{12,8},{16,12},{20,16},{24,20},{28,24},{1,29},{... | collective-permute-start | bytes 5308424 | tf_op jit(solution)/shard_map/ppermute | solution.py:38
  224.3 116.3 %collective-permute-start.4 = (bf16[96,9216]{1,0:T(8,128)(2,1)S(1)}, bf16[96,9216]{1,0:T(8,128)(2,1)S(1)}, u32[]{:S(2)}, u32[]{:S(2)}) collective-permute-start(bf16[96,9216]{1,0:T(8,128)(2,1)S(1)} %collective-permute-done.2), channel_id=1, source_target_pairs={{0,4},{4,8},{8,12},{12,16},{16,20},{20,24},{24,28},{28,0},{1,5},{5... | collective-permute-start | bytes 5308424 | tf_op jit(solution)/shard_map/ppermute | solution.py:31
  244.8 110.0 %collective-permute-start.5 = (bf16[96,9216]{1,0:T(8,128)(2,1)S(1)}, bf16[96,9216]{1,0:T(8,128)(2,1)S(1)}, u32[]{:S(2)}, u32[]{:S(2)}) collective-permute-start(bf16[96,9216]{1,0:T(8,128)(2,1)S(1)} %collective-permute-done.3), channel_id=1, source_target_pairs={{0,28},{4,0},{8,4},{12,8},{16,12},{20,16},{24,20},{28,24},{1,29},{... | collective-permute-start | bytes 5308424 | tf_op jit(solution)/shard_map/ppermute | solution.py:38
  340.7 67.7 %collective-permute-start.6 = (bf16[96,9216]{1,0:T(8,128)(2,1)S(1)}, bf16[96,9216]{1,0:T(8,128)(2,1)S(1)}, u32[]{:S(2)}, u32[]{:S(2)}) collective-permute-start(bf16[96,9216]{1,0:T(8,128)(2,1)S(1)} %collective-permute-done.4), channel_id=1, source_target_pairs={{0,4},{4,8},{8,12},{12,16},{16,20},{20,24},{24,28},{28,0},{1,5},{5... | collective-permute-start | bytes 5308424 | tf_op jit(solution)/shard_map/ppermute | solution.py:31
  344.6 65.2 %copy-start.2 = (bf16[2,64,768]{2,1,0:T(8,128)(2,1)S(1)}, bf16[2,64,768]{2,1,0:T(8,128)(2,1)}, u32[]{:S(2)}) copy-start(bf16[2,64,768]{2,1,0:T(8,128)(2,1)} %param.14) | copy-start | bytes 589828
  422.7 5.6 copy-start.60
  428.3 4.4 copy-start.5
  428.3 4.4 copy-start.35
  428.3 4.4 copy-start.47
  428.3 41.7 %copy-start.41 = (f32[8,50]{1,0:T(8,128)S(1)}, f32[8,50]{1,0:T(8,128)}, u32[]{:S(2)}) copy-start(f32[8,50]{1,0:T(8,128)} %copy-done.40) | copy-start | bytes 4804
  428.3 41.7 %copy-start.46 = (f32[2304]{0:T(1024)S(1)}, f32[2304]{0:T(1024)}, u32[]{:S(2)}) copy-start(f32[2304]{0:T(1024)} %get-tuple-element.124) | copy-start | bytes 27652
  428.3 41.7 %copy-start.58 = (f32[768]{0:T(1024)S(1)}, f32[768]{0:T(1024)}, u32[]{:S(2)}) copy-start(f32[768]{0:T(1024)} %get-tuple-element.121) | copy-start | bytes 9220
  428.3 41.7 %copy-start.59 = (f32[768]{0:T(1024)S(1)}, f32[768]{0:T(1024)}, u32[]{:S(2)}) copy-start(f32[768]{0:T(1024)} %get-tuple-element.122) | copy-start | bytes 9220
  428.3 41.7 %copy-start.61 = (f32[8,50]{1,0:T(8,128)S(1)}, f32[8,50]{1,0:T(8,128)}, u32[]{:S(2)}) copy-start(f32[8,50]{1,0:T(8,128)} %add_rsqrt_fusion.1) | copy-start | bytes 4804
  487.6 4.8 copy-start.7
  487.6 4.8 copy-start.57
  495.1 6.5 copy-start.54
  501.6 55.8 %copy-start.64 = (s32[8]{0:T(128)S(1)}, s32[8]{0:T(128)}, u32[]{:S(2)}) copy-start(s32[8]{0:T(128)} %iota_add_fusion) | copy-start | bytes 100
  604.8 5.3 copy-start.21
  604.8 5.3 copy-start.32
  604.8 5.3 copy-start.37
  610.1 5.0 copy-start.13
  610.1 5.0 copy-start.53
  620.1 5.1 copy-start.14
  620.1 5.1 copy-start.22
  620.1 5.1 copy-start.26
  620.1 5.1 copy-start.33
  620.1 5.1 copy-start.38
  631.1 4.2 copy-start.18
  631.1 4.2 copy-start.24
  631.1 4.2 copy-start.28
  631.1 4.2 copy-start.30
  658.9 636.9 %all-reduce.4.cloned.1.call-start = ((), (), s32[]{:S(2)}) async-start(), calls=%async_computation.3 | async-start | bytes 589824 | tf_op jit(solution)/shard_map/psum | solution.py:391
  1295.8 7.5 copy-start.1
  1303.3 6.1 copy-start.12
  (28 other events, 70.9 us)
Sparse Core Ops, SparseCore 0:
  10.2 394.8 all-gather.2
  659.0 447.3 reduce-scatter.1
  1166.3 129.4 all-reduce.3
